TPU v7x, 32 devices: a whole 2x2x4 slice. The times are simulated.
32 devices in a mesh: fsdp: 8 (over z, x), tp: 4 (over y, core).
Axes of the slice: x: 2, y: 2, z: 4, core: 2. Of those that a mesh axis runs over, the one named last changes fastest.
Arguments:
- tokens: bfloat16 [8, 2048, 768], P('fsdp', 'tp'), may hold values from -6 to 6
- lengths: int32 [8, 4], P('fsdp'), may hold values from 288 to 1024, as said below
- pictures: int32 [8, 2048], P('fsdp'), may hold values from 0 to 3, as said below
- w_query: bfloat16 [768, 768], P('fsdp', 'tp'), may hold values from -0.21875 to 0.21875
- w_key: bfloat16 [768, 768], P('fsdp', 'tp'), may hold values from -0.21875 to 0.21875
- w_value: bfloat16 [768, 768], P('fsdp', 'tp'), may hold values from -0.21875 to 0.21875
- w_out: bfloat16 [768, 768], P('tp', 'fsdp'), may hold values from -0.875 to 0.875
- w_up: bfloat16 [768, 3072], P('fsdp', 'tp'), may hold values from -0.21875 to 0.21875
- w_down: bfloat16 [3072, 768], P('tp', 'fsdp'), may hold values from -0.15625 to 0.15625
- norm1_gain: float32 [768], P(('fsdp', 'tp')), may hold values from 0.5 to 1.5
- norm1_shift: float32 [768], P(('fsdp', 'tp')), may hold values from -1.75 to 1.75
- norm2_gain: float32 [768], P(('fsdp', 'tp')), may hold values from 0.5 to 1.5
- norm2_shift: float32 [768], P(('fsdp', 'tp')), may hold values from -1.75 to 1.75
- query_gain: float32 [768], P(('fsdp', 'tp')), may hold values from 1 to 2
- key_gain: float32 [768], P(('fsdp', 'tp')), may hold values from 1 to 2
- cotangent: bfloat16 [8, 2048, 768], P('fsdp', 'tp'), may hold values from -6 to 6
Outputs:
- layer_out: bfloat16 [8, 2048, 768], P('fsdp', 'tp')
- input_grad: float32 [8, 2048, 768], P('fsdp', 'tp')
- grad_query: float32 [768, 768], P('fsdp', 'tp')
- grad_key: float32 [768, 768], P('fsdp', 'tp')
- grad_value: float32 [768, 768], P('fsdp', 'tp')
- grad_output_proj: float32 [768, 768], P('tp', 'fsdp')
- grad_up: float32 [768, 3072], P('fsdp', 'tp')
- grad_down: float32 [3072, 768], P('tp', 'fsdp')
- grad_norm1_gain: float32 [768], P(('fsdp', 'tp'))
- grad_norm1_shift: float32 [768], P(('fsdp', 'tp'))
- grad_norm2_gain: float32 [768], P(('fsdp', 'tp'))
- grad_norm2_shift: float32 [768], P(('fsdp', 'tp'))
- grad_query_gain: float32 [768], P(('fsdp', 'tp'))
- grad_key_gain: float32 [768], P(('fsdp', 'tp'))
- statistics: float32 [4], replicated
Inputs may be any that keep to these rules, and one draw needn't show every extreme that they name: The lengths of a row sum to at most 2048; one picture of every row has exactly 1024 patches. Slots of a row carry the pictures in order, each picture covering as many slots as its length; slots after the row's total length repeat the last picture's number.
All inputs are finite; a program needn't handle non-finite values.
Results may differ from a plain program's by a relative error of at most 0.018.
Values may be sent and summed in bfloat16 or wider, within the bound.
A program may use at most 192 MiB of HBM per device.

v0:
```python
import jax
import jax.numpy as jnp
from jax import lax
from jax.sharding import PartitionSpec as P

HD = 64
EPS = 1e-06
ROOT_HALF = 0.7071067811865476
DENSITY = 0.3989422804014327


def normalise(values, scaling, offset):
    centre = jnp.mean(values, axis=-1, keepdims=True)
    centred = values - centre
    spread = jnp.mean(centred * centred, axis=-1, keepdims=True)
    inverse = lax.rsqrt(spread + EPS)
    normed = centred * inverse
    return (normed * scaling + offset, normed, inverse)


def normalise_back(grad_out, normed, inverse, scaling):
    grad_unit = grad_out * scaling
    grad_values = inverse * (
        grad_unit
        - jnp.mean(grad_unit, axis=-1, keepdims=True)
        - normed * jnp.mean(grad_unit * normed, axis=-1, keepdims=True)
    )
    return (grad_values, jnp.sum(grad_out * normed, axis=(0, 1)), jnp.sum(grad_out, axis=(0, 1)))


def gelu_slope(values):
    return (
        0.5 * (1.0 + jax.scipy.special.erf(values * ROOT_HALF))
        + values * jnp.exp(-0.5 * values * values) * DENSITY
    )


def gather_tokens(values):
    return lax.all_gather(values, "tp", axis=1, tiled=True)


def gather_grads(values):
    return lax.all_gather(values, "tp", axis=1, tiled=True)


def reduce_tokens(values):
    return lax.psum_scatter(
        values.astype(jnp.bfloat16), "tp", scatter_dimension=1, tiled=True
    ).astype(jnp.float32)


def reduce_grads(values):
    return lax.psum_scatter(
        values.astype(jnp.bfloat16), "tp", scatter_dimension=1, tiled=True
    ).astype(jnp.float32)


def block_scores(query, keyed, picture_query, picture_key, key_mask):
    raw_scores = jnp.einsum("qhd,khd->hqk", query, keyed, preferred_element_type=jnp.float32)
    allowed = (picture_query[:, None] == picture_key[None, :]) & (key_mask[None, :] > 0)
    return jnp.where(allowed[None], raw_scores * query.shape[-1] ** (-0.5), -1e30)


def forward_row(packed):
    query_row, key_row, value_row, picture_row, mask_row = packed
    full_len = query_row.shape[0]
    block_len = min(512, full_len)
    block_count = full_len // block_len

    def forward_one_block(packed_block):
        query_block, picture_block = packed_block
        scores = block_scores(query_block, key_row, picture_block, picture_row, mask_row)
        highest = jnp.max(scores, axis=-1, keepdims=True)
        logsum = highest + jnp.log(jnp.sum(jnp.exp(scores - highest), axis=-1, keepdims=True))
        probability = jnp.exp(scores - logsum).astype(jnp.bfloat16)
        mixture = jnp.einsum(
            "hqk,khd->qhd", probability, value_row, preferred_element_type=jnp.float32
        )
        return (mixture, logsum)

    query_blocks = query_row.reshape((block_count, block_len) + query_row.shape[1:])
    return lax.map(forward_one_block, (query_blocks, picture_row.reshape(block_count, block_len)))


def backward_row(packed):
    query_row, key_row, value_row, picture_row, mask_row, grad_row, logsum_row = packed
    full_len = query_row.shape[0]
    block_len = min(512, full_len)
    block_count = full_len // block_len
    factor = query_row.shape[-1] ** (-0.5)

    def backward_one_block(running, packed_block):
        grad_key, grad_value = running
        query_block, picture_block, grad_block, logsum_block = packed_block
        scores = block_scores(query_block, key_row, picture_block, picture_row, mask_row)
        probability = jnp.exp(scores - logsum_block)
        prob_low = probability.astype(jnp.bfloat16)
        grad_prob = jnp.einsum(
            "qhd,khd->hqk", grad_block, value_row, preferred_element_type=jnp.float32
        )
        grad_value = grad_value + jnp.einsum(
            "hqk,qhd->khd", prob_low, grad_block, preferred_element_type=jnp.float32
        )
        centre = jnp.sum(probability * grad_prob, axis=-1, keepdims=True)
        grad_scores = (probability * (grad_prob - centre)).astype(jnp.bfloat16)
        grad_query = factor * jnp.einsum(
            "hqk,khd->qhd", grad_scores, key_row, preferred_element_type=jnp.float32
        )
        grad_key = grad_key + factor * jnp.einsum(
            "hqk,qhd->khd", grad_scores, query_block, preferred_element_type=jnp.float32
        )
        return ((grad_key, grad_value), grad_query)

    zero_state = jnp.zeros(key_row.shape, jnp.float32)
    block_shape = (block_count, block_len) + query_row.shape[1:]
    (grad_key, grad_value), grad_query = lax.scan(
        backward_one_block,
        (zero_state, zero_state),
        (
            query_row.reshape(block_shape),
            picture_row.reshape(block_count, block_len),
            grad_row.reshape(block_shape),
            logsum_row,
        ),
    )
    return (grad_query.reshape(key_row.shape), grad_key, grad_value)


def local(
    tokens,
    lengths,
    pictures,
    w_query,
    w_key,
    w_value,
    w_out,
    w_up,
    w_down,
    norm1_gain,
    norm1_shift,
    norm2_gain,
    norm2_shift,
    query_gain,
    key_gain,
    cotangent,
):
    tp_place = lax.axis_index("tp")
    local_len = tokens.shape[1]
    model_width = tokens.shape[2]
    full_len = pictures.shape[1]
    local_width = w_query.shape[1]
    heads_local = local_width // HD
    gain_one, shift_one, gain_two, shift_two, gain_query, gain_key = (
        lax.all_gather(norm1_gain, ("fsdp", "tp"), axis=0, tiled=True),
        lax.all_gather(norm1_shift, ("fsdp", "tp"), axis=0, tiled=True),
        lax.all_gather(norm2_gain, ("fsdp", "tp"), axis=0, tiled=True),
        lax.all_gather(norm2_shift, ("fsdp", "tp"), axis=0, tiled=True),
        lax.all_gather(query_gain, ("fsdp", "tp"), axis=0, tiled=True),
        lax.all_gather(key_gain, ("fsdp", "tp"), axis=0, tiled=True),
    )
    positions = jnp.arange(full_len, dtype=jnp.int32)
    valid_full = (positions[None, :] < jnp.sum(lengths, axis=1)[:, None]).astype(jnp.float32)
    valid_here = lax.dynamic_slice_in_dim(valid_full, tp_place * local_len, local_len, 1)[
        :, :, None
    ]
    qgain_here = lax.dynamic_slice_in_dim(
        gain_query, tp_place * local_width, local_width, 0
    ).reshape(heads_local, HD)
    kgain_here = lax.dynamic_slice_in_dim(gain_key, tp_place * local_width, local_width, 0).reshape(
        heads_local, HD
    )
    front_query, front_key, front_value, front_out = (
        lax.all_gather(w_query, "fsdp", axis=0, tiled=True),
        lax.all_gather(w_key, "fsdp", axis=0, tiled=True),
        lax.all_gather(w_value, "fsdp", axis=0, tiled=True),
        lax.all_gather(w_out, "fsdp", axis=1, tiled=True),
    )
    inputs = tokens.astype(jnp.float32)
    hidden, normed_one, inverse_one = normalise(inputs, gain_one, shift_one)
    hidden_full = gather_tokens(hidden.astype(jnp.bfloat16))
    row_shape = hidden_full.shape[:2] + (heads_local, HD)
    query = jnp.dot(hidden_full, front_query, preferred_element_type=jnp.float32).reshape(row_shape)
    keyed = jnp.dot(hidden_full, front_key, preferred_element_type=jnp.float32).reshape(row_shape)
    value_low = (
        jnp.dot(hidden_full, front_value, preferred_element_type=jnp.float32)
        .astype(jnp.bfloat16)
        .reshape(row_shape)
    )
    query_norm, query_unit, query_inverse = normalise(query, qgain_here, 0.0)
    key_norm, key_unit, key_inverse = normalise(keyed, kgain_here, 0.0)
    query_low = query_norm.astype(jnp.bfloat16)
    key_low = key_norm.astype(jnp.bfloat16)
    mixture, logsum = lax.map(forward_row, (query_low, key_low, value_low, pictures, valid_full))
    mixture_low = mixture.reshape(hidden_full.shape[:2] + (local_width,)).astype(jnp.bfloat16)
    attn_branch = valid_here * reduce_tokens(
        jnp.dot(mixture_low, front_out, preferred_element_type=jnp.float32)
    )
    middle = inputs + attn_branch
    hidden_two, normed_two, inverse_two = normalise(middle, gain_two, shift_two)
    hidden_two_full = gather_tokens(hidden_two.astype(jnp.bfloat16))
    front_up, front_down = (
        lax.all_gather(w_up, "fsdp", axis=0, tiled=True),
        lax.all_gather(w_down, "fsdp", axis=1, tiled=True),
    )
    up_value = jnp.dot(hidden_two_full, front_up, preferred_element_type=jnp.float32)
    activated = jax.nn.gelu(up_value, approximate=False).astype(jnp.bfloat16)
    mlp_branch = valid_here * reduce_tokens(
        jnp.dot(activated, front_down, preferred_element_type=jnp.float32)
    )
    result = (middle + mlp_branch).astype(jnp.bfloat16)
    square_sums = jnp.stack(
        [
            jnp.sum(valid_here * inputs * inputs),
            jnp.sum(attn_branch * attn_branch),
            jnp.sum(valid_here * middle * middle),
            jnp.sum(mlp_branch * mlp_branch),
        ]
    )
    valid_count = jnp.sum(valid_here)
    back_up, back_down = (
        lax.all_gather(w_up, "fsdp", axis=0, tiled=True),
        lax.all_gather(w_down, "fsdp", axis=1, tiled=True),
    )
    back_query, back_key, back_value, back_out = (
        lax.all_gather(w_query, "fsdp", axis=0, tiled=True),
        lax.all_gather(w_key, "fsdp", axis=0, tiled=True),
        lax.all_gather(w_value, "fsdp", axis=0, tiled=True),
        lax.all_gather(w_out, "fsdp", axis=1, tiled=True),
    )
    grad_y = cotangent.astype(jnp.float32) * valid_here
    grad_y_full = gather_grads(grad_y.astype(jnp.bfloat16))
    grad_down = jnp.einsum(
        "rlf,rld->fd", activated, grad_y_full, preferred_element_type=jnp.float32
    )
    grad_act = jnp.dot(grad_y_full, back_down.T, preferred_element_type=jnp.float32)
    grad_pre = (grad_act * gelu_slope(up_value)).astype(jnp.bfloat16)
    grad_up = jnp.einsum(
        "rld,rlf->df", hidden_two_full, grad_pre, preferred_element_type=jnp.float32
    )
    grad_hidden_two = reduce_grads(jnp.dot(grad_pre, back_up.T, preferred_element_type=jnp.float32))
    mlp_grads = (
        lax.psum_scatter(grad_up, "fsdp", scatter_dimension=0, tiled=True),
        lax.psum_scatter(grad_down, "fsdp", scatter_dimension=1, tiled=True),
    )
    grad_mid_norm, grad_gain_two, grad_shift_two = normalise_back(
        grad_hidden_two, normed_two, inverse_two, gain_two
    )
    grad_middle = grad_y + grad_mid_norm
    grad_branch_here = (valid_here * grad_middle).astype(jnp.bfloat16)
    grad_branch_full = gather_grads(grad_branch_here)
    grad_out_proj = jnp.einsum(
        "rlh,rld->hd", mixture_low, grad_branch_full, preferred_element_type=jnp.float32
    )
    grad_mixture = jnp.dot(grad_branch_full, back_out.T, preferred_element_type=jnp.float32).astype(
        jnp.bfloat16
    )
    grad_qnorm, grad_knorm, grad_value_full = lax.map(
        backward_row,
        (
            query_low,
            key_low,
            value_low,
            pictures,
            valid_full,
            grad_mixture.reshape(row_shape),
            logsum,
        ),
    )
    grad_query_pre, grad_qgain, unused_one = normalise_back(
        grad_qnorm, query_unit, query_inverse, qgain_here
    )
    grad_key_pre, grad_kgain, unused_two = normalise_back(
        grad_knorm, key_unit, key_inverse, kgain_here
    )
    flat_shape = hidden_full.shape[:2] + (local_width,)
    grad_query_low = grad_query_pre.reshape(flat_shape).astype(jnp.bfloat16)
    grad_key_low = grad_key_pre.reshape(flat_shape).astype(jnp.bfloat16)
    grad_value_low = grad_value_full.reshape(flat_shape).astype(jnp.bfloat16)
    grad_wquery = jnp.einsum(
        "rld,rlh->dh", hidden_full, grad_query_low, preferred_element_type=jnp.float32
    )
    grad_wkey = jnp.einsum(
        "rld,rlh->dh", hidden_full, grad_key_low, preferred_element_type=jnp.float32
    )
    grad_wvalue = jnp.einsum(
        "rld,rlh->dh", hidden_full, grad_value_low, preferred_element_type=jnp.float32
    )
    grad_hidden_part = (
        jnp.dot(grad_query_low, back_query.T, preferred_element_type=jnp.float32)
        + jnp.dot(grad_key_low, back_key.T, preferred_element_type=jnp.float32)
        + jnp.dot(grad_value_low, back_value.T, preferred_element_type=jnp.float32)
    )
    grad_hidden = reduce_grads(grad_hidden_part)
    attn_grads = (
        lax.psum_scatter(grad_wquery, "fsdp", scatter_dimension=0, tiled=True),
        lax.psum_scatter(grad_wkey, "fsdp", scatter_dimension=0, tiled=True),
        lax.psum_scatter(grad_wvalue, "fsdp", scatter_dimension=0, tiled=True),
        lax.psum_scatter(grad_out_proj, "fsdp", scatter_dimension=1, tiled=True),
    )
    grad_in_norm, grad_gain_one, grad_shift_one = normalise_back(
        grad_hidden, normed_one, inverse_one, gain_one
    )
    grad_inputs = grad_middle + grad_in_norm
    zero_width = jnp.zeros((model_width,), jnp.float32)
    grad_qgain_full = lax.dynamic_update_slice_in_dim(
        zero_width, grad_qgain.reshape(local_width), tp_place * local_width, 0
    )
    grad_kgain_full = lax.dynamic_update_slice_in_dim(
        zero_width, grad_kgain.reshape(local_width), tp_place * local_width, 0
    )
    small_shards = (
        lax.psum_scatter(grad_gain_one, ("fsdp", "tp"), scatter_dimension=0, tiled=True),
        lax.psum_scatter(grad_shift_one, ("fsdp", "tp"), scatter_dimension=0, tiled=True),
        lax.psum_scatter(grad_gain_two, ("fsdp", "tp"), scatter_dimension=0, tiled=True),
        lax.psum_scatter(grad_shift_two, ("fsdp", "tp"), scatter_dimension=0, tiled=True),
        lax.psum_scatter(grad_qgain_full, ("fsdp", "tp"), scatter_dimension=0, tiled=True),
        lax.psum_scatter(grad_kgain_full, ("fsdp", "tp"), scatter_dimension=0, tiled=True),
    )
    totals, counted = lax.psum((square_sums, valid_count), ("fsdp", "tp"))
    statistics = jnp.sqrt(totals / (counted * model_width))
    return (
        result,
        grad_inputs,
        attn_grads[0],
        attn_grads[1],
        attn_grads[2],
        attn_grads[3],
        mlp_grads[0],
        mlp_grads[1],
        small_shards[0],
        small_shards[1],
        small_shards[2],
        small_shards[3],
        small_shards[4],
        small_shards[5],
        statistics,
    )


def solution(mesh):
    in_specs = (
        P("fsdp", "tp", None),
        P("fsdp", None),
        P("fsdp", None),
        P("fsdp", "tp"),
        P("fsdp", "tp"),
        P("fsdp", "tp"),
        P("tp", "fsdp"),
        P("fsdp", "tp"),
        P("tp", "fsdp"),
        P(("fsdp", "tp")),
        P(("fsdp", "tp")),
        P(("fsdp", "tp")),
        P(("fsdp", "tp")),
        P(("fsdp", "tp")),
        P(("fsdp", "tp")),
        P("fsdp", "tp", None),
    )
    out_specs = (
        P("fsdp", "tp", None),
        P("fsdp", "tp", None),
        P("fsdp", "tp"),
        P("fsdp", "tp"),
        P("fsdp", "tp"),
        P("tp", "fsdp"),
        P("fsdp", "tp"),
        P("tp", "fsdp"),
        P(("fsdp", "tp")),
        P(("fsdp", "tp")),
        P(("fsdp", "tp")),
        P(("fsdp", "tp")),
        P(("fsdp", "tp")),
        P(("fsdp", "tp")),
        P(),
    )
    return jax.shard_map(local, mesh=mesh, in_specs=in_specs, out_specs=out_specs, check_vma=False)
```

profile of v0, /device:TPU:0, one launch (start us, length us, event | category | flops | bytes accessed | tf_op | source)
XLA Modules:
  0.0 1174.1 jit_solution(14461486698308457316)
XLA Ops:
  16.0 42.4 %all-reduce.13 = (f32[768]{0:T(1024)}, f32[768]{0:T(1024)}, f32[768]{0:T(1024)S(1)}, f32[768]{0:T(1024)S(1)}, f32[768]{0:T(1024)S(1)}, /*index=5*/f32[768]{0:T(1024)S(1)}) all-reduce(f32[768]{0:T(1024)S(1)} %dynamic-update-slice.5, f32[768]{0:T(1024)S(1)} %dynamic-update-slice.4, ...), channel_id=1, replica_groups=mesh['fsdp'=8,'tp'=4] {'fsdp','tp'}, use_global_device_ids=true, to_apply=%add.5 | all-reduce | flops 4608 | bytes 36864
  63.4 31.0 %all_gather.62 = bf16[192,768]{0,1:T(8,128)(2,1)S(1)} all-gather(bf16[192,96]{0,1:T(8,128)(2,1)S(1)} %copy.45), channel_id=1, replica_groups=mesh['fsdp'=8,'tp'=4] {'fsdp'}, dimensions={1}, use_global_device_ids=true | all-gather | bytes 331776 | tf_op jit(solution)/shard_map/all_gather | solution.py:176
  94.4 31.2 %all_gather.57 = bf16[768,192]{1,0:T(8,128)(2,1)S(1)} all-gather(bf16[96,192]{1,0:T(8,128)(2,1)S(1)} %copy-done.54), channel_id=1, replica_groups=mesh['fsdp'=8,'tp'=4] {'fsdp'}, dimensions={0}, use_global_device_ids=true | all-gather | bytes 331776 | tf_op jit(solution)/shard_map/all_gather | solution.py:173
  125.7 31.1 %all_gather.59 = bf16[768,192]{1,0:T(8,128)(2,1)S(1)} all-gather(bf16[96,192]{1,0:T(8,128)(2,1)S(1)} %copy-done.55), channel_id=1, replica_groups=mesh['fsdp'=8,'tp'=4] {'fsdp'}, dimensions={0}, use_global_device_ids=true | all-gather | bytes 331776 | tf_op jit(solution)/shard_map/all_gather | solution.py:174
  156.8 33.0 %all_gather.61 = bf16[768,192]{1,0:T(8,128)(2,1)} all-gather(bf16[96,192]{1,0:T(8,128)(2,1)S(1)} %copy-done.56), channel_id=1, replica_groups=mesh['fsdp'=8,'tp'=4] {'fsdp'}, dimensions={0}, use_global_device_ids=true | all-gather | bytes 331776 | tf_op jit(solution)/shard_map/all_gather | solution.py:175
  205.3 92.3 %while.50 = (s32[]{:T(128)}, bf16[4,512,3,64]{1,3,2,0:T(8,128)(2,1)}, f32[4,3,512,1]{2,1,3,0:T(4,128)}, s32[4,512]{1,0:T(4,128)S(1)}, s32[2048]{0:T(1024)S(1)}, ...) while((s32[]{:T(128)}, ...), condition=%wide.region_10.11_spmd.clone.clone, body=%wide.region_7.10_spmd.clone.sunk.clone | while | flops 842011136 | bytes 50469040 | solution.py:82
  304.1 36.6 %reduce-scatter.13.cloned.1.call-done = bf16[1,512,768]{2,1,0:T(8,128)(2,1)} async-done(((bf16[1,2048,768]{2,1,0:T(8,128)(2,1)}), bf16[1,512,768]{2,1,0:T(8,128)(2,1)}) %reduce-scatter.13.cloned.1.call-update) | async-done | bytes 786448 | tf_op jit(solution)/shard_map/reduce_scatter | solution.py:47
  349.9 27.1 %all-gather.9.cloned.1.call-done = bf16[1,2048,768]{2,1,0:T(8,128)(2,1)} async-done(((bf16[1,512,768]{2,1,0:T(8,128)(2,1)}), bf16[1,2048,768]{2,1,0:T(8,128)(2,1)}) %all-gather.9.cloned.1.call-update) | async-done | bytes 3145744 | tf_op jit(solution)/shard_map/all_gather | solution.py:39
  377.0 18.6 %fusion.47 = (bf16[2048,768]{1,0:T(8,128)(2,1)}, f32[2048,768]{1,0:T(8,128)}) fusion(bf16[768,768]{1,0:T(8,128)(2,1)} %all-gather.11.cloned.1.call-done, bf16[1,2048,768]{2,1,0:T(8,128)(2,1)} %all-gather.9.cloned.1.call-done), kind=kOutput, calls=%fused_computation.61 | convolution fusion | flops 2518155264 | bytes 13762560 | tf_op jit(solution)/shard_map/dot_general | solution.py:205
  395.6 25.2 %all-gather.13.cloned.1.call-done = bf16[768,768]{0,1:T(8,128)(2,1)} async-done(((bf16[768,96]{0,1:T(8,128)(2,1)}), bf16[768,768]{0,1:T(8,128)(2,1)}) %all-gather.13.cloned.1.call-update) | async-done | bytes 1179664 | tf_op jit(solution)/shard_map/all_gather | solution.py:203
  420.9 29.1 %all-gather.15.cloned.1.call-done = bf16[1,2048,768]{2,1,0:T(8,128)(2,1)} async-done(((bf16[1,512,768]{2,1,0:T(8,128)(2,1)}), bf16[1,2048,768]{2,1,0:T(8,128)(2,1)}) %all-gather.15.cloned.1.call-update) | async-done | bytes 3145744 | tf_op jit(solution)/shard_map/all_gather | solution.py:43
  469.0 31.4 %reduce-scatter.17.cloned.1.call-done = bf16[1,512,768]{2,1,0:T(8,128)(2,1)} async-done(((bf16[1,2048,768]{2,1,0:T(8,128)(2,1)}), bf16[1,512,768]{2,1,0:T(8,128)(2,1)}) %reduce-scatter.17.cloned.1.call-update) | async-done | bytes 786448 | tf_op jit(solution)/shard_map/reduce_scatter | solution.py:53
  500.5 40.4 %reduce-scatter.15.cloned.1.call-done = bf16[1,512,768]{2,1,0:T(8,128)(2,1)} async-done(((bf16[1,2048,768]{2,1,0:T(8,128)(2,1)}), bf16[1,512,768]{2,1,0:T(8,128)(2,1)}) %reduce-scatter.15.cloned.1.call-update) | async-done | bytes 786448 | tf_op jit(solution)/shard_map/reduce_scatter | solution.py:47
  547.6 28.4 %all-gather.17.cloned.1.call-done = bf16[1,2048,768]{2,1,0:T(8,128)(2,1)} async-done(((bf16[1,512,768]{2,1,0:T(8,128)(2,1)}), bf16[1,2048,768]{2,1,0:T(8,128)(2,1)}) %all-gather.17.cloned.1.call-update) | async-done | bytes 3145744 | tf_op jit(solution)/shard_map/all_gather | solution.py:43
  579.9 132.6 %while.51 = (s32[]{:T(128)}, f32[2048,3,64]{0,2,1:T(8,128)}, f32[2048,3,64]{0,2,1:T(8,128)}, f32[4,512,3,64]{1,3,2,0:T(8,128)}, bf16[4,512,3,64]{1,3,2,0:T(8,128...) while((s32[]{:T(128)}, f32[2048,3,64]{0,2,1:T(8,128)}, ...), condition=%wide.region_20.21_spmd.clone.clone, body=%wide.region_18.20_spmd.clone.sunk.clone | while | flops 2064617984 | bytes 169277904 | solution.py:116
  738.3 7.1 fusion.65
  760.5 23.0 %reduce-scatter.31.cloned.1.call-done = f32[96,192]{1,0:T(8,128)} async-done(((f32[768,192]{1,0:T(8,128)}), f32[96,192]{1,0:T(8,128)}) %reduce-scatter.31.cloned.1.call-update) | async-done | bytes 73744
  785.1 37.7 %reduce-scatter.19.cloned.1.call-done = bf16[1,512,768]{2,1,0:T(8,128)(2,1)} async-done(((bf16[1,2048,768]{2,1,0:T(8,128)(2,1)}), bf16[1,512,768]{2,1,0:T(8,128)(2,1)}) %reduce-scatter.19.cloned.1.call-update) | async-done | bytes 786448 | tf_op jit(solution)/shard_map/reduce_scatter | solution.py:53
  824.8 41.4 %all-reduce.12 = (f32[768]{0:T(1024)S(1)}, f32[768]{0:T(1024)S(1)}, f32[768]{0:T(1024)S(1)}, f32[768]{0:T(1024)S(1)}, f32[768]{0:T(1024)S(1)}, /*index=5*/f32[768]{0:T(1024)S(1)}, f32[4]{0:T(128)S(1)}, f32[]{:T(128)}) all-reduce(f32[768]{0:T(1024)S(1)} %get-tuple-element.306, ...), channel_id=12, replica_groups=mesh['fsdp'=8,'tp'=4] {'fsdp','tp'}, use_global_device_ids=true, to_apply=%region_35.36.clone | all-reduce | flops 4613 | bytes 36904
  873.7 23.4 %reduce-scatter.27.cloned.1.call-done = f32[96,768]{1,0:T(8,128)} async-done(((f32[768,768]{1,0:T(8,128)}), f32[96,768]{1,0:T(8,128)}) %reduce-scatter.27.cloned.1.call-update) | async-done | bytes 294928 | tf_op jit(solution)/shard_map/reduce_scatter | solution.py:242
  897.1 72.5 %reduce-scatter.29.cloned.1.call-done = f32[768,96]{0,1:T(8,128)} async-done(((f32[768,768]{0,1:T(8,128)}), f32[768,96]{0,1:T(8,128)}) %reduce-scatter.29.cloned.1.call-update) | async-done | bytes 294928 | tf_op jit(solution)/shard_map/reduce_scatter | solution.py:243
  969.5 65.8 %reduce-scatter.23.cloned.1.call-done = f32[96,192]{1,0:T(8,128)} async-done(((f32[768,192]{1,0:T(8,128)}), f32[96,192]{1,0:T(8,128)}) %reduce-scatter.23.cloned.1.call-update) | async-done | bytes 73744 | tf_op jit(solution)/shard_map/reduce_scatter | solution.py:296
  1035.4 65.4 %reduce-scatter.25.cloned.1.call-done = f32[96,192]{1,0:T(8,128)} async-done(((f32[768,192]{1,0:T(8,128)}), f32[96,192]{1,0:T(8,128)}) %reduce-scatter.25.cloned.1.call-update) | async-done | bytes 73744 | tf_op jit(solution)/shard_map/reduce_scatter | solution.py:297
  1100.7 65.8 %reduce-scatter.21.cloned.1.call-done = f32[96,192]{1,0:T(8,128)} async-done(((f32[768,192]{1,0:T(8,128)}), f32[96,192]{1,0:T(8,128)}) %reduce-scatter.21.cloned.1.call-update) | async-done | bytes 73744 | tf_op jit(solution)/shard_map/reduce_scatter | solution.py:295
  (434 shorter events, 347.5 us)
Async XLA Ops:
  8.1 148.7 %copy-start.56 = (bf16[96,192]{1,0:T(8,128)(2,1)S(1)}, bf16[96,192]{1,0:T(8,128)(2,1)}, u32[]{:S(2)}) copy-start(bf16[96,192]{1,0:T(8,128)(2,1)} %param.25) | copy-start | bytes 110596
  8.1 182.6 %all-gather.7.cloned.1.call-start = ((), (), s32[]{:S(2)}) async-start(), calls=%async_computation.10 | async-start | bytes 3932160 | tf_op jit(solution)/shard_map/all_gather | solution.py:39
  11.0 182.8 %copy-start.64 = (f32[512]{0:T(512)}, f32[512]{0:T(512)S(1)}, u32[]{:S(2)}) copy-start(f32[512]{0:T(512)S(1)} %add_rsqrt_fusion.3) | copy-start | bytes 6148
  58.4 135.4 %copy-start.58 = (f32[768]{0:T(1024)}, f32[768]{0:T(1024)S(1)}, u32[]{:S(2)}) copy-start(f32[768]{0:T(1024)S(1)} %get-tuple-element.372) | copy-start | bytes 9220
  60.8 279.9 %reduce-scatter.13.cloned.1.call-start = ((), (), s32[]{:S(2)}) async-start(), calls=%async_computation.11 | async-start | bytes 3932160 | tf_op jit(solution)/shard_map/reduce_scatter | solution.py:47
  61.7 138.2 %copy-start.62 = (f32[3,64]{1,0:T(4,128)}, f32[3,64]{1,0:T(4,128)S(1)}, u32[]{:S(2)}) copy-start(f32[3,64]{1,0:T(4,128)S(1)} %mul.406) | copy-start | bytes 2308
  62.1 138.2 %copy-start.68 = (f32[3,64]{1,0:T(4,128)}, f32[3,64]{1,0:T(4,128)S(1)}, u32[]{:S(2)}) copy-start(f32[3,64]{1,0:T(4,128)S(1)} %mul.400) | copy-start | bytes 2308
  302.2 47.7 %all-gather.11.cloned.1.call-start = ((), (), s32[]{:S(2)}) async-start(), calls=%async_computation.13 | async-start | bytes 1327104 | tf_op jit(solution)/shard_map/all_gather | solution.py:202
  302.8 74.2 %all-gather.9.cloned.1.call-start = ((), (), s32[]{:S(2)}) async-start(), calls=%async_computation.12 | async-start | bytes 3932160 | tf_op jit(solution)/shard_map/all_gather | solution.py:39
  348.5 72.3 %all-gather.13.cloned.1.call-start = ((), (), s32[]{:S(2)}) async-start(), calls=%async_computation.14 | async-start | bytes 1327104 | tf_op jit(solution)/shard_map/all_gather | solution.py:203
  349.1 100.9 %all-gather.15.cloned.1.call-start = ((), (), s32[]{:S(2)}) async-start(), calls=%async_computation.16 | async-start | bytes 3932160 | tf_op jit(solution)/shard_map/all_gather | solution.py:43
  349.8 150.6 %reduce-scatter.17.cloned.1.call-start = ((), (), s32[]{:S(2)}) async-start(), calls=%async_computation.17 | async-start | bytes 3932160 | tf_op jit(solution)/shard_map/reduce_scatter | solution.py:53
  462.4 78.5 %reduce-scatter.15.cloned.1.call-start = ((), (), s32[]{:S(2)}) async-start(), calls=%async_computation.15 | async-start | bytes 3932160 | tf_op jit(solution)/shard_map/reduce_scatter | solution.py:47
  469.0 107.0 %all-gather.17.cloned.1.call-start = ((), (), s32[]{:S(2)}) async-start(), calls=%async_computation.18 | async-start | bytes 3932160 | tf_op jit(solution)/shard_map/all_gather | solution.py:43
  547.5 235.9 %reduce-scatter.31.cloned.1.call-start = ((), (), s32[]{:S(2)}) async-start(), calls=%async_computation.25 | async-start | bytes 884736
  579.8 132.7 %copy-start.41 = (f32[2048,3]{0,1:T(4,128)S(1)}, f32[2048,3]{0,1:T(4,128)}, u32[]{:S(2)}) copy-start(f32[2048,3]{0,1:T(4,128)} %copy-done.40) | copy-start | bytes 73732
  579.9 132.7 %copy-start.45 = (f32[2048,3]{0,1:T(4,128)S(1)}, f32[2048,3]{0,1:T(4,128)}, u32[]{:S(2)}) copy-start(f32[2048,3]{0,1:T(4,128)} %copy-done.44) | copy-start | bytes 73732
  579.9 132.7 %copy-start.69 = (f32[3,64]{1,0:T(4,128)S(1)}, f32[3,64]{1,0:T(4,128)}, u32[]{:S(2)}) copy-start(f32[3,64]{1,0:T(4,128)} %copy-done.68) | copy-start | bytes 2308
  720.8 101.9 %reduce-scatter.19.cloned.1.call-start = ((), (), s32[]{:S(2)}) async-start(), calls=%async_computation.19 | async-start | bytes 3932160 | tf_op jit(solution)/shard_map/reduce_scatter | solution.py:53
  730.0 167.0 %reduce-scatter.27.cloned.1.call-start = ((), (), s32[]{:S(2)}) async-start(), calls=%async_computation.23 | async-start | bytes 2654208 | tf_op jit(solution)/shard_map/reduce_scatter | solution.py:242
  738.0 231.6 %reduce-scatter.29.cloned.1.call-start = ((), (), s32[]{:S(2)}) async-start(), calls=%async_computation.24 | async-start | bytes 2654208 | tf_op jit(solution)/shard_map/reduce_scatter | solution.py:243
  745.4 289.9 %reduce-scatter.23.cloned.1.call-start = ((), (), s32[]{:S(2)}) async-start(), calls=%async_computation.21 | async-start | bytes 884736 | tf_op jit(solution)/shard_map/reduce_scatter | solution.py:296
  748.6 352.1 %reduce-scatter.25.cloned.1.call-start = ((), (), s32[]{:S(2)}) async-start(), calls=%async_computation.22 | async-start | bytes 884736 | tf_op jit(solution)/shard_map/reduce_scatter | solution.py:297
  751.7 414.8 %reduce-scatter.21.cloned.1.call-start = ((), (), s32[]{:S(2)}) async-start(), calls=%async_computation.20 | async-start | bytes 884736 | tf_op jit(solution)/shard_map/reduce_scatter | solution.py:295
  (107 other events, 1461.1 us)
Sparse Core Ops, SparseCore 0:
  60.9 28.6 all-gather.6
  302.3 38.2 reduce-scatter.12
  462.5 37.9 reduce-scatter.16
  502.9 37.9 reduce-scatter.14
Sparse Core Ops, SparseCore 1:
  305.1 41.8 all-gather.10
  348.6 28.3 all-gather.8
  379.3 41.5 all-gather.12
  423.1 26.8 all-gather.14
  547.6 28.3 all-gather.16
  720.9 62.5 reduce-scatter.30
  785.9 36.9 reduce-scatter.18
  827.1 69.9 reduce-scatter.26
  901.4 68.1 reduce-scatter.28
  973.8 61.5 reduce-scatter.22
  1039.1 61.6 reduce-scatter.24
  1105.0 61.5 reduce-scatter.20
where the time goes:
time: 1180 us; the launch traced here: 1170 us
  waiting for transfers between devices  574 us (49%)
  matrix products  225 us (19%)
  blocking collectives  210 us (18%)
  other arithmetic  103 us (9%)
  local copies, waits for them, and re-layouts  42 us (4%)
  between operations  17.5 us (1%)
    unnamed x2, blocking collectives  83.7 us
    reduce_scatter x2, waiting for transfers between devices, reduce_tokens(): lax.psum_scatter(values.astype(jnp.bfloat16), 'tp', scatter_dimension=1,...  77 us
    reduce_scatter x1, waiting for transfers between devices, local(): lax.psum_scatter(grad_down, 'fsdp', scatter_dimension=1, tiled=True)  72.5 us
    reduce_scatter x2, waiting for transfers between devices, reduce_grads(): lax.psum_scatter(values.astype(jnp.bfloat16), 'tp', scatter_dimension=1,...  69.1 us
    reduce_scatter x1, waiting for transfers between devices, local(): lax.psum_scatter(grad_wkey, 'fsdp', scatter_dimension=0, tiled=True)  65.8 us
    reduce_scatter x1, waiting for transfers between devices, local(): lax.psum_scatter(grad_wquery, 'fsdp', scatter_dimension=0, tiled=True)  65.8 us
    reduce_scatter x1, waiting for transfers between devices, local(): lax.psum_scatter(grad_wvalue, 'fsdp', scatter_dimension=0, tiled=True)  65.4 us
    all_gather x2, waiting for transfers between devices, gather_grads(): return lax.all_gather(values, 'tp', axis=1, tiled=True)  57.5 us
  transfers between devices with their start and end apart: 16, of which 14 were waited for; matrix products, arithmetic and copies ran while one was open for 7% of the time, Pallas kernels for 0%

commit v1 on v0

--- a/solution.py
+++ b/solution.py
@@ -7,6 +7,22 @@
 EPS = 1e-06
 ROOT_HALF = 0.7071067811865476
 DENSITY = 0.3989422804014327
+
+
+def ring_gather(x, axis, dim):
+    ways, here, step = (lax.axis_size(axis), lax.axis_index(axis), x.shape[dim])
+    lengths = [n * ways if d == dim else n for d, n in enumerate(x.shape)]
+    full = lax.dynamic_update_slice_in_dim(jnp.zeros(lengths, x.dtype), x, here * step, axis=dim)
+    going_up = going_down = x
+    for far in range(1, ways // 2 + 1):
+        going_up = lax.ppermute(going_up, axis, [(d, (d + 1) % ways) for d in range(ways)])
+        full = lax.dynamic_update_slice_in_dim(full, going_up, (here - far) % ways * step, axis=dim)
+        if 2 * far < ways:
+            going_down = lax.ppermute(going_down, axis, [(d, (d - 1) % ways) for d in range(ways)])
+            full = lax.dynamic_update_slice_in_dim(
+                full, going_down, (here + far) % ways * step, axis=dim
+            )
+    return full
 
 
 def normalise(values, scaling, offset):
@@ -173,7 +189,7 @@
         lax.all_gather(w_query, "fsdp", axis=0, tiled=True),
         lax.all_gather(w_key, "fsdp", axis=0, tiled=True),
         lax.all_gather(w_value, "fsdp", axis=0, tiled=True),
-        lax.all_gather(w_out, "fsdp", axis=1, tiled=True),
+        ring_gather(w_out, "fsdp", 1),
     )
     inputs = tokens.astype(jnp.float32)
     hidden, normed_one, inverse_one = normalise(inputs, gain_one, shift_one)

time: 1180 us -> 1170 us (level)
  waiting for transfers between devices: 574 us -> 549 us
  starting transfers between devices: 0.94 us -> 15.2 us
    all_gather x2, waiting for transfers between devices: 57.5 us -> 29.1 us  [gather_grads(): return lax.all_gather(values, 'tp', axis=1, tiled=True)]
    ppermute x0 -> x7, starting transfers between devices: none -> 14.2 us  [the longest x3 11.9 us: ring_gather(): lax.ppermute(going_down, axis, [(d, (d - 1) % ways) for d in range(ways)])]
  transfers between devices with their start and end apart: 16 -> 23, of which waited for: 14 -> 14; matrix products, arithmetic and copies ran while one was open for 7% -> 7% of each run, Pallas kernels for 0% -> 0%
where the time goes in v1:
time: 1170 us; the launch traced here: 1160 us
  waiting for transfers between devices  549 us (47%)
  matrix products  225 us (19%)
  blocking collectives  209 us (18%)
  other arithmetic  103 us (9%)
  local copies, waits for them, and re-layouts  44.9 us (4%)
  between operations  17.6 us (2%)
  starting transfers between devices  15.2 us (1%)
    unnamed x2, blocking collectives  84.1 us
    reduce_scatter x2, waiting for transfers between devices, reduce_tokens(): lax.psum_scatter(values.astype(jnp.bfloat16), 'tp', scatter_dimension=1,...  79.6 us
    reduce_scatter x1, waiting for transfers between devices, local(): lax.psum_scatter(grad_down, 'fsdp', scatter_dimension=1, tiled=True)  72.5 us
    reduce_scatter x2, waiting for transfers between devices, reduce_grads(): lax.psum_scatter(values.astype(jnp.bfloat16), 'tp', scatter_dimension=1,...  69.1 us
    reduce_scatter x1, waiting for transfers between devices, local(): lax.psum_scatter(grad_wkey, 'fsdp', scatter_dimension=0, tiled=True)  65.9 us
    reduce_scatter x1, waiting for transfers between devices, local(): lax.psum_scatter(grad_wquery, 'fsdp', scatter_dimension=0, tiled=True)  65.8 us
    reduce_scatter x1, waiting for transfers between devices, local(): lax.psum_scatter(grad_wvalue, 'fsdp', scatter_dimension=0, tiled=True)  65.4 us
    dot_general x8, matrix products, block_scores(): jnp.einsum('qhd,khd->hqk', query, keyed, preferred_element_type=jnp.float32)  38.9 us
  transfers between devices with their start and end apart: 23, of which 14 were waited for; matrix products, arithmetic and copies ran while one was open for 7% of the time, Pallas kernels for 0%

profile of v1, /device:TPU:0, one launch (start us, length us, event | category | flops | bytes accessed | tf_op | source)
XLA Modules:
  0.0 1164.5 jit_solution(11157167689089633207)
XLA Ops:
  16.0 42.4 %all-reduce.13 = (f32[768]{0:T(1024)}, f32[768]{0:T(1024)}, f32[768]{0:T(1024)S(1)}, f32[768]{0:T(1024)S(1)}, f32[768]{0:T(1024)S(1)}, /*index=5*/f32[768]{0:T(1024)S(1)}) all-reduce(f32[768]{0:T(1024)S(1)} %dynamic-update-slice.5, f32[768]{0:T(1024)S(1)} %dynamic-update-slice.4, ...), channel_id=1, replica_groups=mesh['fsdp'=8,'tp'=4] {'fsdp','tp'}, use_global_device_ids=true, to_apply=%add.5 | all-reduce | flops 4608 | bytes 36864
  67.8 31.1 %all_gather.56 = bf16[768,192]{1,0:T(8,128)(2,1)S(1)} all-gather(bf16[96,192]{1,0:T(8,128)(2,1)S(1)} %copy-done.54), channel_id=1, replica_groups=mesh['fsdp'=8,'tp'=4] {'fsdp'}, dimensions={0}, use_global_device_ids=true | all-gather | bytes 331776 | tf_op jit(solution)/shard_map/all_gather | solution.py:189
  103.7 31.1 %all_gather.58 = bf16[768,192]{1,0:T(8,128)(2,1)S(1)} all-gather(bf16[96,192]{1,0:T(8,128)(2,1)S(1)} %copy-done.55), channel_id=1, replica_groups=mesh['fsdp'=8,'tp'=4] {'fsdp'}, dimensions={0}, use_global_device_ids=true | all-gather | bytes 331776 | tf_op jit(solution)/shard_map/all_gather | solution.py:190
  139.5 31.5 %all_gather.60 = bf16[768,192]{1,0:T(8,128)(2,1)S(1)} all-gather(bf16[96,192]{1,0:T(8,128)(2,1)S(1)} %copy-done.56), channel_id=1, replica_groups=mesh['fsdp'=8,'tp'=4] {'fsdp'}, dimensions={0}, use_global_device_ids=true | all-gather | bytes 331776 | tf_op jit(solution)/shard_map/all_gather | solution.py:191
  191.6 91.9 %while.50 = (s32[]{:T(128)}, bf16[4,512,3,64]{1,3,2,0:T(8,128)(2,1)}, f32[4,3,512,1]{2,1,3,0:T(4,128)}, s32[4,512]{1,0:T(4,128)S(1)}, s32[2048]{0:T(1024)S(1)}, ...) while((s32[]{:T(128)}, ...), condition=%wide.region_10.11_spmd.clone.clone, body=%wide.region_7.10_spmd.clone.sunk.clone | while | flops 842011136 | bytes 50469040 | solution.py:98
  200.0 6.8 exponential_reduce_fusion.3
  289.5 39.2 %reduce-scatter.13.cloned.1.call-done = bf16[1,512,768]{2,1,0:T(8,128)(2,1)} async-done(((bf16[1,2048,768]{2,1,0:T(8,128)(2,1)}), bf16[1,512,768]{2,1,0:T(8,128)(2,1)}) %reduce-scatter.13.cloned.1.call-update) | async-done | bytes 786448 | tf_op jit(solution)/shard_map/reduce_scatter | solution.py:63
  337.3 27.1 %all-gather.9.cloned.1.call-done = bf16[1,2048,768]{2,1,0:T(8,128)(2,1)} async-done(((bf16[1,512,768]{2,1,0:T(8,128)(2,1)}), bf16[1,2048,768]{2,1,0:T(8,128)(2,1)}) %all-gather.9.cloned.1.call-update) | async-done | bytes 3145744 | tf_op jit(solution)/shard_map/all_gather | solution.py:55
  364.4 18.5 %fusion.47 = (bf16[2048,768]{1,0:T(8,128)(2,1)}, f32[2048,768]{1,0:T(8,128)}) fusion(bf16[768,768]{1,0:T(8,128)(2,1)} %all-gather.11.cloned.1.call-done, bf16[1,2048,768]{2,1,0:T(8,128)(2,1)} %all-gather.9.cloned.1.call-done), kind=kOutput, calls=%fused_computation.61 | convolution fusion | flops 2518155264 | bytes 13762560 | tf_op jit(solution)/shard_map/dot_general | solution.py:221
  383.0 25.3 %all-gather.13.cloned.1.call-done = bf16[768,768]{0,1:T(8,128)(2,1)} async-done(((bf16[768,96]{0,1:T(8,128)(2,1)}), bf16[768,768]{0,1:T(8,128)(2,1)}) %all-gather.13.cloned.1.call-update) | async-done | bytes 1179664 | tf_op jit(solution)/shard_map/all_gather | solution.py:219
  408.3 29.1 %all-gather.15.cloned.1.call-done = bf16[1,2048,768]{2,1,0:T(8,128)(2,1)} async-done(((bf16[1,512,768]{2,1,0:T(8,128)(2,1)}), bf16[1,2048,768]{2,1,0:T(8,128)(2,1)}) %all-gather.15.cloned.1.call-update) | async-done | bytes 3145744 | tf_op jit(solution)/shard_map/all_gather | solution.py:59
  456.4 31.4 %reduce-scatter.17.cloned.1.call-done = bf16[1,512,768]{2,1,0:T(8,128)(2,1)} async-done(((bf16[1,2048,768]{2,1,0:T(8,128)(2,1)}), bf16[1,512,768]{2,1,0:T(8,128)(2,1)}) %reduce-scatter.17.cloned.1.call-update) | async-done | bytes 786448 | tf_op jit(solution)/shard_map/reduce_scatter | solution.py:69
  487.9 40.4 %reduce-scatter.15.cloned.1.call-done = bf16[1,512,768]{2,1,0:T(8,128)(2,1)} async-done(((bf16[1,2048,768]{2,1,0:T(8,128)(2,1)}), bf16[1,512,768]{2,1,0:T(8,128)(2,1)}) %reduce-scatter.15.cloned.1.call-update) | async-done | bytes 786448 | tf_op jit(solution)/shard_map/reduce_scatter | solution.py:63
  535.1 31.2 %all_gather.68 = bf16[192,768]{0,1:T(8,128)(2,1)S(1)} all-gather(bf16[192,96]{0,1:T(8,128)(2,1)S(1)} %copy.45), channel_id=1, replica_groups=mesh['fsdp'=8,'tp'=4] {'fsdp'}, dimensions={1}, use_global_device_ids=true | all-gather | bytes 331776 | tf_op jit(solution)/shard_map/all_gather | solution.py:244
  570.1 132.6 %while.51 = (s32[]{:T(128)}, f32[2048,3,64]{0,2,1:T(8,128)}, f32[2048,3,64]{0,2,1:T(8,128)}, f32[4,512,3,64]{1,3,2,0:T(8,128)}, bf16[4,512,3,64]{1,3,2,0:T(8,128...) while((s32[]{:T(128)}, f32[2048,3,64]{0,2,1:T(8,128)}, ...), condition=%wide.region_20.21_spmd.clone.clone, body=%wide.region_18.20_spmd.clone.sunk.clone | while | flops 2064617984 | bytes 169277904 | solution.py:132
  728.5 7.1 fusion.65
  750.6 23.0 %reduce-scatter.31.cloned.1.call-done = f32[96,192]{1,0:T(8,128)} async-done(((f32[768,192]{1,0:T(8,128)}), f32[96,192]{1,0:T(8,128)}) %reduce-scatter.31.cloned.1.call-update) | async-done | bytes 73744
  775.3 37.7 %reduce-scatter.19.cloned.1.call-done = bf16[1,512,768]{2,1,0:T(8,128)(2,1)} async-done(((bf16[1,2048,768]{2,1,0:T(8,128)(2,1)}), bf16[1,512,768]{2,1,0:T(8,128)(2,1)}) %reduce-scatter.19.cloned.1.call-update) | async-done | bytes 786448 | tf_op jit(solution)/shard_map/reduce_scatter | solution.py:69
  814.9 41.7 %all-reduce.12 = (f32[768]{0:T(1024)S(1)}, f32[768]{0:T(1024)S(1)}, f32[768]{0:T(1024)S(1)}, f32[768]{0:T(1024)S(1)}, f32[768]{0:T(1024)S(1)}, /*index=5*/f32[768]{0:T(1024)S(1)}, f32[4]{0:T(128)S(1)}, f32[]{:T(128)}) all-reduce(f32[768]{0:T(1024)S(1)} %get-tuple-element.306, ...), channel_id=12, replica_groups=mesh['fsdp'=8,'tp'=4] {'fsdp','tp'}, use_global_device_ids=true, to_apply=%region_35.36.clone | all-reduce | flops 4613 | bytes 36904
  864.2 23.0 %reduce-scatter.27.cloned.1.call-done = f32[96,768]{1,0:T(8,128)} async-done(((f32[768,768]{1,0:T(8,128)}), f32[96,768]{1,0:T(8,128)}) %reduce-scatter.27.cloned.1.call-update) | async-done | bytes 294928 | tf_op jit(solution)/shard_map/reduce_scatter | solution.py:258
  887.2 72.5 %reduce-scatter.29.cloned.1.call-done = f32[768,96]{0,1:T(8,128)} async-done(((f32[768,768]{0,1:T(8,128)}), f32[768,96]{0,1:T(8,128)}) %reduce-scatter.29.cloned.1.call-update) | async-done | bytes 294928 | tf_op jit(solution)/shard_map/reduce_scatter | solution.py:259
  959.7 65.9 %reduce-scatter.23.cloned.1.call-done = f32[96,192]{1,0:T(8,128)} async-done(((f32[768,192]{1,0:T(8,128)}), f32[96,192]{1,0:T(8,128)}) %reduce-scatter.23.cloned.1.call-update) | async-done | bytes 73744 | tf_op jit(solution)/shard_map/reduce_scatter | solution.py:312
  1025.7 65.4 %reduce-scatter.25.cloned.1.call-done = f32[96,192]{1,0:T(8,128)} async-done(((f32[768,192]{1,0:T(8,128)}), f32[96,192]{1,0:T(8,128)}) %reduce-scatter.25.cloned.1.call-update) | async-done | bytes 73744 | tf_op jit(solution)/shard_map/reduce_scatter | solution.py:313
  1091.1 65.8 %reduce-scatter.21.cloned.1.call-done = f32[96,192]{1,0:T(8,128)} async-done(((f32[768,192]{1,0:T(8,128)}), f32[96,192]{1,0:T(8,128)}) %reduce-scatter.21.cloned.1.call-update) | async-done | bytes 73744 | tf_op jit(solution)/shard_map/reduce_scatter | solution.py:311
  (449 shorter events, 358.1 us)
Async XLA Ops:
  8.1 169.0 %all-gather.7.cloned.1.call-start = ((), (), s32[]{:S(2)}) async-start(), calls=%async_computation.10 | async-start | bytes 3932160 | tf_op jit(solution)/shard_map/all_gather | solution.py:55
  9.5 165.6 %copy-start.52 = (f32[512]{0:T(512)}, f32[512]{0:T(512)S(1)}, u32[]{:S(2)}) copy-start(f32[512]{0:T(512)S(1)} %broadcast_multiply_fusion.11) | copy-start | bytes 6148
  60.8 267.9 %reduce-scatter.13.cloned.1.call-start = ((), (), s32[]{:S(2)}) async-start(), calls=%async_computation.11 | async-start | bytes 3932160 | tf_op jit(solution)/shard_map/reduce_scatter | solution.py:63
  60.8 6.9 collective-permute-start
  63.2 35.7 %collective-permute-start.1 = (bf16[192,96]{1,0:T(8,128)(2,1)S(1)}, bf16[192,96]{1,0:T(8,128)(2,1)S(1)}, u32[]{:S(2)}, u32[]{:S(2)}) collective-permute-start(bf16[192,96]{1,0:T(8,128)(2,1)S(1)} %copy-done.50), channel_id=1, source_target_pairs={{0,28},{4,0},{8,4},{12,8},{16,12},{20,16},{24,20},{28,24},{1,29},{... | collective-permute-start | bytes 110600 | tf_op jit(solution)/shard_map/ppermute | solution.py:21
  67.8 35.9 %collective-permute-start.2 = (bf16[192,96]{1,0:T(8,128)(2,1)S(1)}, bf16[192,96]{1,0:T(8,128)(2,1)S(1)}, u32[]{:S(2)}, u32[]{:S(2)}) collective-permute-start(bf16[192,96]{1,0:T(8,128)(2,1)S(1)} %collective-permute-done), channel_id=1, source_target_pairs={{0,4},{4,8},{8,12},{12,16},{16,20},{20,24},{24,28},{28,0},{1,5},{5... | collective-permute-start | bytes 110600 | tf_op jit(solution)/shard_map/ppermute | solution.py:18
  98.9 35.9 %collective-permute-start.3 = (bf16[192,96]{1,0:T(8,128)(2,1)S(1)}, bf16[192,96]{1,0:T(8,128)(2,1)S(1)}, u32[]{:S(2)}, u32[]{:S(2)}) collective-permute-start(bf16[192,96]{1,0:T(8,128)(2,1)S(1)} %collective-permute-done.1), channel_id=1, source_target_pairs={{0,28},{4,0},{8,4},{12,8},{16,12},{20,16},{24,20},{28,24},{1,29},{... | collective-permute-start | bytes 110600 | tf_op jit(solution)/shard_map/ppermute | solution.py:21
  103.7 35.8 %collective-permute-start.4 = (bf16[192,96]{1,0:T(8,128)(2,1)S(1)}, bf16[192,96]{1,0:T(8,128)(2,1)S(1)}, u32[]{:S(2)}, u32[]{:S(2)}) collective-permute-start(bf16[192,96]{1,0:T(8,128)(2,1)S(1)} %collective-permute-done.2), channel_id=1, source_target_pairs={{0,4},{4,8},{8,12},{12,16},{16,20},{20,24},{24,28},{28,0},{1,5},{5... | collective-permute-start | bytes 110600 | tf_op jit(solution)/shard_map/ppermute | solution.py:18
  134.8 41.4 %collective-permute-start.5 = (bf16[192,96]{1,0:T(8,128)(2,1)S(1)}, bf16[192,96]{1,0:T(8,128)(2,1)S(1)}, u32[]{:S(2)}, u32[]{:S(2)}) collective-permute-start(bf16[192,96]{1,0:T(8,128)(2,1)S(1)} %collective-permute-done.3), channel_id=1, source_target_pairs={{0,28},{4,0},{8,4},{12,8},{16,12},{20,16},{24,20},{28,24},{1,29},{... | collective-permute-start | bytes 110600 | tf_op jit(solution)/shard_map/ppermute | solution.py:21
  139.5 37.3 %collective-permute-start.6 = (bf16[192,96]{1,0:T(8,128)(2,1)S(1)}, bf16[192,96]{1,0:T(8,128)(2,1)S(1)}, u32[]{:S(2)}, u32[]{:S(2)}) collective-permute-start(bf16[192,96]{1,0:T(8,128)(2,1)S(1)} %collective-permute-done.4), channel_id=1, source_target_pairs={{0,4},{4,8},{8,12},{12,16},{16,20},{20,24},{24,28},{28,0},{1,5},{5... | collective-permute-start | bytes 110600 | tf_op jit(solution)/shard_map/ppermute | solution.py:18
  288.2 49.1 %all-gather.11.cloned.1.call-start = ((), (), s32[]{:S(2)}) async-start(), calls=%async_computation.13 | async-start | bytes 1327104 | tf_op jit(solution)/shard_map/all_gather | solution.py:218
  288.8 75.6 %all-gather.9.cloned.1.call-start = ((), (), s32[]{:S(2)}) async-start(), calls=%async_computation.12 | async-start | bytes 3932160 | tf_op jit(solution)/shard_map/all_gather | solution.py:55
  335.9 72.3 %all-gather.13.cloned.1.call-start = ((), (), s32[]{:S(2)}) async-start(), calls=%async_computation.14 | async-start | bytes 1327104 | tf_op jit(solution)/shard_map/all_gather | solution.py:219
  336.5 100.9 %all-gather.15.cloned.1.call-start = ((), (), s32[]{:S(2)}) async-start(), calls=%async_computation.16 | async-start | bytes 3932160 | tf_op jit(solution)/shard_map/all_gather | solution.py:59
  337.3 150.6 %reduce-scatter.17.cloned.1.call-start = ((), (), s32[]{:S(2)}) async-start(), calls=%async_computation.17 | async-start | bytes 3932160 | tf_op jit(solution)/shard_map/reduce_scatter | solution.py:69
  449.8 78.5 %reduce-scatter.15.cloned.1.call-start = ((), (), s32[]{:S(2)}) async-start(), calls=%async_computation.15 | async-start | bytes 3932160 | tf_op jit(solution)/shard_map/reduce_scatter | solution.py:63
  456.4 109.9 %all-gather.17.cloned.1.call-start = ((), (), s32[]{:S(2)}) async-start(), calls=%async_computation.18 | async-start | bytes 3932160 | tf_op jit(solution)/shard_map/all_gather | solution.py:59
  534.9 238.7 %reduce-scatter.31.cloned.1.call-start = ((), (), s32[]{:S(2)}) async-start(), calls=%async_computation.25 | async-start | bytes 884736
  711.1 101.9 %reduce-scatter.19.cloned.1.call-start = ((), (), s32[]{:S(2)}) async-start(), calls=%async_computation.19 | async-start | bytes 3932160 | tf_op jit(solution)/shard_map/reduce_scatter | solution.py:69
  720.2 167.0 %reduce-scatter.27.cloned.1.call-start = ((), (), s32[]{:S(2)}) async-start(), calls=%async_computation.23 | async-start | bytes 2654208 | tf_op jit(solution)/shard_map/reduce_scatter | solution.py:258
  728.2 231.6 %reduce-scatter.29.cloned.1.call-start = ((), (), s32[]{:S(2)}) async-start(), calls=%async_computation.24 | async-start | bytes 2654208 | tf_op jit(solution)/shard_map/reduce_scatter | solution.py:259
  735.6 290.1 %reduce-scatter.23.cloned.1.call-start = ((), (), s32[]{:S(2)}) async-start(), calls=%async_computation.21 | async-start | bytes 884736 | tf_op jit(solution)/shard_map/reduce_scatter | solution.py:312
  738.8 352.3 %reduce-scatter.25.cloned.1.call-start = ((), (), s32[]{:S(2)}) async-start(), calls=%async_computation.22 | async-start | bytes 884736 | tf_op jit(solution)/shard_map/reduce_scatter | solution.py:313
  741.9 415.0 %reduce-scatter.21.cloned.1.call-start = ((), (), s32[]{:S(2)}) async-start(), calls=%async_computation.20 | async-start | bytes 884736 | tf_op jit(solution)/shard_map/reduce_scatter | solution.py:311
  (110 other events, 2521.5 us)
Sparse Core Ops, SparseCore 0:
  60.9 28.6 all-gather.6
  288.3 40.3 reduce-scatter.12
  449.9 37.9 reduce-scatter.16
  490.3 37.9 reduce-scatter.14
Sparse Core Ops, SparseCore 1:
  291.1 43.8 all-gather.10
  336.5 27.8 all-gather.8
  366.7 41.5 all-gather.12
  410.5 26.8 all-gather.14
  535.0 28.3 all-gather.16
  711.1 62.4 reduce-scatter.30
  776.0 36.8 reduce-scatter.18
  817.3 69.9 reduce-scatter.26
  891.6 68.1 reduce-scatter.28
  964.0 61.6 reduce-scatter.22
  1029.4 61.6 reduce-scatter.24
  1095.3 61.5 reduce-scatter.20
